TPU v7x, 32 devices: a whole 2x2x4 slice. The times are simulated.
32 devices in a mesh: ctx: 8 (over y, x, core), fsdp: 4 (over z).
Axes of the slice: x: 2, y: 2, z: 4, core: 2. Of those that a mesh axis runs over, the one named last changes fastest.
Arguments:
- tokens: bfloat16 [4, 4096, 768], P('fsdp', 'ctx'), may hold values from -6 to 6
- cotangent: bfloat16 [4, 4096, 768], P('fsdp', 'ctx'), may hold values from -6 to 6
- lengths: int32 [4, 4], P('fsdp'), may hold values from 1 to 2048, 4096 in all within a row
- dealing: int32 [4, 16], P('fsdp'), may hold values from 0 to 15, each once within a row
- qkv_weight: bfloat16 [768, 2304], P('fsdp'), may hold values from -0.21875 to 0.21875
- out_weight: bfloat16 [768, 768], P('fsdp'), may hold values from -0.21875 to 0.21875
- in_weight: bfloat16 [768, 3072], P('fsdp'), may hold values from -0.21875 to 0.21875
- back_weight: bfloat16 [3072, 768], P('fsdp'), may hold values from -0.109375 to 0.109375
- norm_gains: bfloat16 [3, 768], P(None, 'fsdp'), may hold values from 0.25 to 1.75
- shifts: bfloat16 [7, 768], P(None, 'fsdp'), may hold values from -1.796875 to 1.796875
- ffn_gain: bfloat16 [3072], P('fsdp'), may hold values from 0.25 to 1.75
- ffn_shifts: bfloat16 [2, 3072], P(None, 'fsdp'), may hold values from -1.796875 to 1.796875
Outputs:
- mixed_out: bfloat16 [4, 4096, 768], P('fsdp', 'ctx')
- input_grad: float32 [4, 4096, 768], P('fsdp', 'ctx')
- qkv_grad: float32 [768, 2304], P(('ctx', 'fsdp'))
- out_grad: float32 [768, 768], P(('ctx', 'fsdp'))
- in_grad: float32 [768, 3072], P(('ctx', 'fsdp'))
- back_grad: float32 [3072, 768], P(('ctx', 'fsdp'))
- gains_grad: float32 [3, 768], P(None, ('ctx', 'fsdp'))
- shifts_grad: float32 [7, 768], P(None, ('ctx', 'fsdp'))
- ffn_gain_grad: float32 [3072], P(('ctx', 'fsdp'))
- ffn_shifts_grad: float32 [2, 3072], P(None, ('ctx', 'fsdp'))
Inputs may be any that keep to these rules, and one draw needn't show every extreme that they name: `lengths`: each row sums to 4096 and its largest entry is exactly 2048. `dealing`: each row is a permutation of the group numbers.
All inputs are finite; a program needn't handle non-finite values.
Results may differ from a plain program's by a relative error of at most 0.018.
Values may be sent and summed in bfloat16 or wider, within the bound.
No kernel may reach another device: no remote copies, remote signals or barrier semaphores. Data moves between devices by JAX's collectives and lax.ppermute only.
A program may use at most 256 MiB of HBM per device.

v0:
```python
import math
import jax
import jax.numpy as jnp
from jax import lax
from jax.sharding import PartitionSpec as P

D = 768
H = 12
DH = 64


def layer_norm(values, gain, shift):
    average = jnp.mean(values, axis=-1, keepdims=True)
    centred = values - average
    variance = jnp.mean(centred * centred, axis=-1, keepdims=True)
    return centred * lax.rsqrt(variance + 1e-05) * gain + shift


def gelu_exact(values):
    return jax.nn.gelu(values, approximate=False)


def row_places(first_row, row_count, deal_row, bounds, group_rows):
    row_ids = first_row + jnp.arange(row_count, dtype=jnp.int32)
    group_ids = row_ids // group_rows
    onehot = (group_ids[:, None] == jnp.arange(deal_row.shape[0], dtype=jnp.int32)[None, :]).astype(
        jnp.int32
    )
    picked = jnp.sum(onehot * deal_row[None, :], axis=1)
    places = picked * group_rows + row_ids % group_rows
    segment = jnp.sum((places[:, None] >= bounds[None, :]).astype(jnp.int32), axis=1)
    return (places, segment)


def outer_sum(left, right):
    return lax.dot_general(
        left, right, (((0,), (0,)), ((), ())), preferred_element_type=jnp.float32
    )


def times_transposed(left, matrix):
    return lax.dot_general(
        left, matrix, (((1,), (1,)), ((), ())), preferred_element_type=jnp.float32
    )


def unpack(loaded):
    qkv_w, out_w, in_w, back_w, gains, shift_rows, ffn_gain, ffn_shift_rows = loaded
    return (
        qkv_w,
        out_w,
        in_w,
        back_w,
        gains.astype(jnp.float32),
        shift_rows.astype(jnp.float32),
        ffn_gain.astype(jnp.float32),
        ffn_shift_rows.astype(jnp.float32),
    )


def local(
    tokens,
    cotangent,
    lengths,
    dealing,
    qkv_weight,
    out_weight,
    in_weight,
    back_weight,
    norm_gains,
    shifts,
    ffn_gain,
    ffn_shifts,
):
    position = lax.axis_index("ctx")
    tok_rows = tokens.shape[1]
    group_rows = tok_rows // 2
    deal_row = dealing[0]
    bounds = jnp.cumsum(lengths[0])
    scaling = DH ** (-0.5)
    loaded = (
        lax.all_gather(qkv_weight, "fsdp", axis=0, tiled=True),
        lax.all_gather(out_weight, "fsdp", axis=0, tiled=True),
        lax.all_gather(in_weight, "fsdp", axis=0, tiled=True),
        lax.all_gather(back_weight, "fsdp", axis=0, tiled=True),
        lax.all_gather(norm_gains, "fsdp", axis=1, tiled=True),
        lax.all_gather(shifts, "fsdp", axis=1, tiled=True),
        lax.all_gather(ffn_gain, "fsdp", axis=0, tiled=True),
        lax.all_gather(ffn_shifts, "fsdp", axis=1, tiled=True),
    )
    qkv_w, out_w, in_w, back_w, gains, shift_rows, ffn_scale, ffn_shift_rows = unpack(loaded)
    inputs = tokens[0].astype(jnp.float32)
    normed = layer_norm(inputs, gains[0], shift_rows[0])
    normed_low = normed.astype(jnp.bfloat16)
    projected = jnp.dot(normed_low, qkv_w, preferred_element_type=jnp.float32)
    query = (projected[:, :D] + shift_rows[1]).astype(jnp.bfloat16)
    keyed = projected[:, D : 2 * D].astype(jnp.bfloat16)
    valued = (projected[:, 2 * D :] + shift_rows[2]).astype(jnp.bfloat16)
    query3 = query.reshape(tok_rows, H, DH)
    q_places, q_segment = row_places(position * tok_rows, tok_rows, deal_row, bounds, group_rows)

    def allowed_pairs(qp, qs, k_places, k_segment):
        return ((k_segment[None, :] == qs[:, None]) & (k_places[None, :] <= qp[:, None]))[None]

    initial = (
        jnp.full((H, tok_rows), -1e30, jnp.float32),
        jnp.zeros((H, tok_rows), jnp.float32),
        jnp.zeros((H, tok_rows, DH), jnp.float32),
    )
    key_rows = lax.all_gather(keyed, "ctx", axis=0, tiled=True)
    value_rows = lax.all_gather(valued, "ctx", axis=0, tiled=True)
    key_count = key_rows.shape[0]
    block_rows = 512
    block_count = key_count // block_rows
    k_places, k_segment = row_places(jnp.int32(0), key_count, deal_row, bounds, group_rows)
    stacked = (
        key_rows.reshape(block_count, block_rows, H, DH),
        value_rows.reshape(block_count, block_rows, H, DH),
        k_places.reshape(block_count, block_rows),
        k_segment.reshape(block_count, block_rows),
    )

    def visit_block(inner_state, pieces):
        maxima, totals, weighted = inner_state
        key3, value3, block_places, block_segment = pieces
        scores = (
            jnp.einsum("qhd,khd->hqk", query3, key3, preferred_element_type=jnp.float32) * scaling
        )
        allowed = allowed_pairs(q_places, q_segment, block_places, block_segment)
        masked = jnp.where(allowed, scores, -1e30)
        raised = jnp.maximum(maxima, jnp.max(masked, axis=-1))
        rescale = jnp.exp(maxima - raised)
        expo = jnp.where(allowed, jnp.exp(masked - raised[..., None]), 0.0)
        totals = totals * rescale + jnp.sum(expo, axis=-1)
        weighted = weighted * rescale[..., None] + jnp.einsum(
            "hqk,khd->hqd", expo.astype(jnp.bfloat16), value3, preferred_element_type=jnp.float32
        )
        return ((raised, totals, weighted), None)

    maxima, totals, weighted = lax.scan(visit_block, initial, stacked)[0]
    context3 = weighted / totals[..., None]
    log_total = maxima + jnp.log(totals)
    context = context3.transpose(1, 0, 2).reshape(tok_rows, D)
    inner = layer_norm(context, gains[1], shift_rows[3])
    inner_low = inner.astype(jnp.bfloat16)
    branch = jnp.dot(inner_low, out_w, preferred_element_type=jnp.float32) + shift_rows[4]
    middle = inputs + branch
    normed_two = layer_norm(middle, gains[2], shift_rows[5])
    normed_two_low = normed_two.astype(jnp.bfloat16)
    hidden = jnp.dot(normed_two_low, in_w, preferred_element_type=jnp.float32) + ffn_shift_rows[0]
    activated = gelu_exact(hidden)
    inner_two = layer_norm(activated, ffn_scale, ffn_shift_rows[1])
    inner_two_low = inner_two.astype(jnp.bfloat16)
    result = jnp.dot(inner_two_low, back_w, preferred_element_type=jnp.float32) + shift_rows[6]
    mixed_out = (middle + result).astype(jnp.bfloat16)
    loaded_back = (
        lax.all_gather(qkv_weight, "fsdp", axis=0, tiled=True),
        lax.all_gather(out_weight, "fsdp", axis=0, tiled=True),
        lax.all_gather(in_weight, "fsdp", axis=0, tiled=True),
        lax.all_gather(back_weight, "fsdp", axis=0, tiled=True),
        lax.all_gather(norm_gains, "fsdp", axis=1, tiled=True),
        lax.all_gather(shifts, "fsdp", axis=1, tiled=True),
        lax.all_gather(ffn_gain, "fsdp", axis=0, tiled=True),
        lax.all_gather(ffn_shifts, "fsdp", axis=1, tiled=True),
    )
    qkv_w, out_w, in_w, back_w, gains, shift_rows, ffn_scale, ffn_shift_rows = unpack(loaded_back)
    upstream = cotangent[0].astype(jnp.float32)
    result_low = cotangent[0]
    grad_back_w = outer_sum(inner_two_low, result_low)
    grad_back_bias = jnp.sum(result_low.astype(jnp.float32), axis=0)
    grad_inner_two = times_transposed(result_low, back_w)
    norm_pull = jax.vjp(layer_norm, activated, ffn_scale, ffn_shift_rows[1])[1]
    grad_activated, grad_ffn_gain, grad_ffn_shift = norm_pull(grad_inner_two)
    gelu_pull = jax.vjp(gelu_exact, hidden)[1]
    grad_hidden = gelu_pull(grad_activated)[0]
    hidden_low = grad_hidden.astype(jnp.bfloat16)
    grad_in_w = outer_sum(normed_two_low, hidden_low)
    grad_in_bias = jnp.sum(hidden_low.astype(jnp.float32), axis=0)
    grad_normed_two = times_transposed(hidden_low, in_w)
    second_pull = jax.vjp(layer_norm, middle, gains[2], shift_rows[5])[1]
    grad_middle_part, grad_gain_two, grad_shift_five = second_pull(grad_normed_two)
    grad_middle = upstream + grad_middle_part
    branch_low = grad_middle.astype(jnp.bfloat16)
    grad_out_w = outer_sum(inner_low, branch_low)
    grad_out_bias = jnp.sum(branch_low.astype(jnp.float32), axis=0)
    grad_inner = times_transposed(branch_low, out_w)
    inner_pull = jax.vjp(layer_norm, context, gains[1], shift_rows[3])[1]
    grad_context, grad_gain_one, grad_shift_three = inner_pull(grad_inner)
    context_grad_low = grad_context.astype(jnp.bfloat16).reshape(tok_rows, H, DH)
    delta = jnp.einsum("qhd,hqd->hq", context_grad_low.astype(jnp.float32), context3)

    def grad_pair(
        q_rows, grad_rows, lse_rows, delta_rows, qp, qs, key3, value3, k_places, k_segment
    ):
        scores = (
            jnp.einsum("qhd,khd->hqk", q_rows, key3, preferred_element_type=jnp.float32) * scaling
        )
        allowed = allowed_pairs(qp, qs, k_places, k_segment)
        probabilities = jnp.where(allowed, jnp.exp(scores - lse_rows[..., None]), 0.0)
        upstream_probs = jnp.einsum(
            "qhd,khd->hqk", grad_rows, value3, preferred_element_type=jnp.float32
        )
        score_grad = (probabilities * (upstream_probs - delta_rows[..., None])).astype(jnp.bfloat16)
        query_add = (
            jnp.einsum("hqk,khd->qhd", score_grad, key3, preferred_element_type=jnp.float32)
            * scaling
        )
        key_add = (
            jnp.einsum("hqk,qhd->khd", score_grad, q_rows, preferred_element_type=jnp.float32)
            * scaling
        )
        value_add = jnp.einsum(
            "hqk,qhd->khd",
            probabilities.astype(jnp.bfloat16),
            grad_rows,
            preferred_element_type=jnp.float32,
        )
        return (query_add, key_add, value_add)

    def grad_block(key3, value3, k_places, k_segment):
        return grad_pair(
            query3,
            context_grad_low,
            log_total,
            delta,
            q_places,
            q_segment,
            key3,
            value3,
            k_places,
            k_segment,
        )

    zero_query = jnp.zeros((tok_rows, H, DH), jnp.float32)
    gathered_keys, gathered_values = (
        lax.all_gather(keyed, "ctx", axis=0, tiled=True),
        lax.all_gather(valued, "ctx", axis=0, tiled=True),
    )
    stream_rows = gathered_keys.shape[0]
    block_rows = math.gcd(stream_rows, 512)
    block_count = stream_rows // block_rows
    all_places, all_segment = row_places(0, stream_rows, deal_row, bounds, group_rows)

    def sweep(query_grad, pieces):
        key3, value3, block_places, block_segment = pieces
        query_add, key_add, value_add = grad_block(key3, value3, block_places, block_segment)
        return (query_grad + query_add, (key_add, value_add))

    query_grad, (key_parts, value_parts) = lax.scan(
        sweep,
        zero_query,
        (
            gathered_keys.reshape(block_count, block_rows, H, DH),
            gathered_values.reshape(block_count, block_rows, H, DH),
            all_places.reshape(block_count, block_rows),
            all_segment.reshape(block_count, block_rows),
        ),
    )
    key_terms = key_parts.reshape(stream_rows, D)
    value_terms = value_parts.reshape(stream_rows, D)
    key_grad_mine, value_grad_mine = (
        lax.psum_scatter(
            key_terms.astype(jnp.bfloat16), "ctx", scatter_dimension=0, tiled=True
        ).astype(jnp.float32),
        lax.psum_scatter(
            value_terms.astype(jnp.bfloat16), "ctx", scatter_dimension=0, tiled=True
        ).astype(jnp.float32),
    )
    qkv_grad_low = jnp.concatenate(
        [query_grad.reshape(tok_rows, D), key_grad_mine, value_grad_mine], axis=1
    ).astype(jnp.bfloat16)
    grad_qkv_w = outer_sum(normed_low, qkv_grad_low)
    column_sums = jnp.sum(qkv_grad_low.astype(jnp.float32), axis=0)
    grad_query_bias = column_sums[:D]
    grad_value_bias = column_sums[2 * D :]
    grad_normed = times_transposed(qkv_grad_low, qkv_w)
    first_pull = jax.vjp(layer_norm, inputs, gains[0], shift_rows[0])[1]
    grad_inputs_part, grad_gain_zero, grad_shift_zero = first_pull(grad_normed)
    input_grad = grad_middle + grad_inputs_part
    gains_terms = jnp.stack([grad_gain_zero, grad_gain_one, grad_gain_two])
    shift_terms = jnp.stack(
        [
            grad_shift_zero,
            grad_query_bias,
            grad_value_bias,
            grad_shift_three,
            grad_out_bias,
            grad_shift_five,
            grad_back_bias,
        ]
    )
    ffn_shift_terms = jnp.stack([grad_in_bias, grad_ffn_shift])
    reduced = (
        lax.psum_scatter(grad_qkv_w, ("ctx", "fsdp"), scatter_dimension=0, tiled=True),
        lax.psum_scatter(grad_out_w, ("ctx", "fsdp"), scatter_dimension=0, tiled=True),
        lax.psum_scatter(grad_in_w, ("ctx", "fsdp"), scatter_dimension=0, tiled=True),
        lax.psum_scatter(grad_back_w, ("ctx", "fsdp"), scatter_dimension=0, tiled=True),
        lax.psum_scatter(gains_terms, ("ctx", "fsdp"), scatter_dimension=1, tiled=True),
        lax.psum_scatter(shift_terms, ("ctx", "fsdp"), scatter_dimension=1, tiled=True),
        lax.psum_scatter(grad_ffn_gain, ("ctx", "fsdp"), scatter_dimension=0, tiled=True),
        lax.psum_scatter(ffn_shift_terms, ("ctx", "fsdp"), scatter_dimension=1, tiled=True),
    )
    return (mixed_out[None], input_grad[None]) + tuple(reduced)


def solution(mesh):
    in_specs = (
        P("fsdp", "ctx", None),
        P("fsdp", "ctx", None),
        P("fsdp", None),
        P("fsdp", None),
        P("fsdp", None),
        P("fsdp", None),
        P("fsdp", None),
        P("fsdp", None),
        P(None, "fsdp"),
        P(None, "fsdp"),
        P("fsdp"),
        P(None, "fsdp"),
    )
    out_specs = (
        P("fsdp", "ctx", None),
        P("fsdp", "ctx", None),
        P(("ctx", "fsdp"), None),
        P(("ctx", "fsdp"), None),
        P(("ctx", "fsdp"), None),
        P(("ctx", "fsdp"), None),
        P(None, ("ctx", "fsdp")),
        P(None, ("ctx", "fsdp")),
        P(("ctx", "fsdp")),
        P(None, ("ctx", "fsdp")),
    )
    return jax.shard_map(local, mesh=mesh, in_specs=in_specs, out_specs=out_specs, check_vma=False)
```

profile of v0, /device:TPU:0, one launch (start us, length us, event | category | flops | bytes accessed | tf_op | source)
XLA Modules:
  0.0 1461.5 jit_solution(8794208688010352200)
XLA Ops:
  8.0 14.9 %all-gather.1 = bf16[4,192,7]{1,2,0:T(8,128)(2,1)S(1)} all-gather(bf16[1,192,7]{1,2,0:T(8,128)(2,1)} %bitcast.267), channel_id=1, replica_groups=mesh['ctx'=8,'fsdp'=4] {'fsdp'}, dimensions={0}, use_global_device_ids=true | all-gather | bytes 13440 | tf_op jit(solution)/shard_map/all_gather | solution.py:87
  23.0 12.2 all-gather
  38.9 43.6 %all-gather.10.cloned.1.call-done = bf16[768,2304]{1,0:T(8,128)(2,1)} async-done(((bf16[192,2304]{1,0:T(8,128)(2,1)}), bf16[768,2304]{1,0:T(8,128)(2,1)}) %all-gather.10.cloned.1.call-update) | async-done | bytes 3538960 | tf_op jit(solution)/shard_map/all_gather | solution.py:82
  95.8 13.0 all_gather.45
  109.5 13.6 all-gather.2
  124.2 10.1 all-gather.12.cloned.1.call-done
  134.3 8.6 copy.91
  142.9 7.5 copy.120
  155.3 26.5 %all-gather.14.cloned.1.call-done = bf16[4096,768]{1,0:T(8,128)(2,1)} async-done(((bf16[512,768]{1,0:T(8,128)(2,1)}), bf16[4096,768]{1,0:T(8,128)(2,1)}) %all-gather.14.cloned.1.call-update) | async-done | bytes 6291472 | tf_op jit(solution)/shard_map/all_gather | solution.py:111
  181.8 8.9 copy.93
  190.7 7.1 copy.121
  202.6 179.3 %while.30 = (s32[]{:T(128)}, f32[12,512]{1,0:T(8,128)S(1)}, f32[12,512]{1,0:T(8,128)S(1)}, f32[12,512,64]{1,2,0:T(8,128)}, s32[8,512]{1,0:T(8,128)S(1)}, /*index...) while((s32[]{:T(128)}, f32[12,512]{1,0:T(8,128)S(1)}, ...), condition=%wide.region_10.11_spmd.clone, body=%wide.region_7.10_spmd.clone.sunk | while | flops 848197632 | bytes 95043760 | solution.py:140
  202.9 8.0 fusion.150
  210.9 7.7 fusion.151
  225.0 8.0 fusion.150
  233.0 7.7 fusion.151
  247.4 8.0 fusion.150
  255.5 7.7 fusion.151
  269.9 8.0 fusion.150
  277.9 7.6 fusion.151
  292.3 8.0 fusion.150
  300.3 7.7 fusion.151
  314.7 8.0 fusion.150
  322.7 7.7 fusion.151
  337.1 8.0 fusion.150
  345.2 7.7 fusion.151
  359.6 8.0 fusion.150
  367.6 7.6 fusion.151
  389.9 21.5 %fusion.101 = (f32[512]{0:T(512)S(1)}, f32[512,3072]{1,0:T(8,128)}, f32[512,3072]{1,0:T(8,128)}, f32[512,3072]{1,0:T(8,128)}) fusion(f32[3072]{0:T(1024)S(1)} %bitcast.261, bf16[768,3072]{1,0:T(8,128)(2,1)} %all-gather.18.cloned.1.call-done, f32[512,768]{1,0:T(8,128)} %copy-done.10, f32[768]{0:T(1024)S(1)} %get-tuple-element.371, ...), kind=kOutput, calls=%fused_computation.205 | convolution fusion | flops 2521693696 | bytes 25190400 | tf_op jit(solution)/shard_map/dot_general | solution.py:150
  411.4 7.4 multiply_reduce_fusion.1
  422.2 10.8 convert_reduce_fusion
  434.6 6.0 multiply_reduce_fusion.3
  447.7 251.0 %while.31 = (s32[]{:T(128)}, f32[512,12,64]{0,2,1:T(8,128)}, bf16[8,512,12,64]{1,3,2,0:T(8,128)(2,1)}, bf16[8,512,12,64]{1,3,2,0:T(8,128)(2,1)}, bf16[8,512,12,6...) while((s32[]{:T(128)}, f32[512,12,64]{0,2,1:T(8,128)}, ...), condition=%wide.region_24.25_spmd.clone, body=%wide.region_23.24_spmd.clone.sunk | while | flops 2047082496 | bytes 195125520 | solution.py:249
  455.7 8.4 fusion.165
  486.7 8.4 fusion.165
  495.1 5.9 bitcast_add_fusion.2
  518.1 8.4 fusion.165
  526.5 5.9 bitcast_add_fusion.2
  549.4 8.4 fusion.165
  557.9 5.9 bitcast_add_fusion.2
  580.8 8.4 fusion.165
  589.3 5.9 bitcast_add_fusion.2
  612.1 8.4 fusion.165
  620.6 5.9 bitcast_add_fusion.2
  643.5 8.4 fusion.165
  652.0 5.9 bitcast_add_fusion.2
  674.9 8.4 fusion.165
  683.4 5.9 bitcast_add_fusion.2
  698.7 6.9 copy.101
  705.6 6.8 copy.123
  712.9 6.9 copy.100
  719.8 7.1 copy.122
  733.2 7.2 fusion.95
  742.3 6.2 fusion.66
  750.1 24.5 %reduce-scatter.14.cloned.1.call-done = bf16[512,768]{0,1:T(8,128)(2,1)} async-done(((bf16[4096,768]{0,1:T(8,128)(2,1)}), bf16[512,768]{0,1:T(8,128)(2,1)}) %reduce-scatter.14.cloned.1.call-update) | async-done | bytes 786448 | tf_op jit(solution)/shard_map/reduce_scatter | solution.py:265
  774.6 65.5 %reduce-scatter.12.cloned.1.call-done = bf16[512,768]{0,1:T(8,128)(2,1)} async-done(((bf16[4096,768]{0,1:T(8,128)(2,1)}), bf16[512,768]{0,1:T(8,128)(2,1)}) %reduce-scatter.12.cloned.1.call-update) | async-done | bytes 786448 | tf_op jit(solution)/shard_map/reduce_scatter | solution.py:262
  840.1 6.6 fusion.88
  848.2 6.8 fusion.64
  855.0 87.4 %reduce-scatter.24.cloned.1.call-done = f32[96,2]{1,0:T(8,128)} async-done(((f32[3072,2]{1,0:T(8,128)}), f32[96,2]{1,0:T(8,128)}) %reduce-scatter.24.cloned.1.call-update) | async-done | bytes 784
  952.3 40.7 %all-reduce.3 = (f32[3,768]{1,0:T(4,128)S(1)}, f32[7,768]{1,0:T(8,128)S(1)}, f32[3072]{0:T(1024)S(1)}) all-reduce(f32[3,768]{1,0:T(4,128)S(1)} %pad_maximum_fusion.2, f32[7,768]{1,0:T(8,128)S(1)} %stack.36, f32[3072]{0:T(1024)S(1)} %copy-done.25), channel_id=8, replica_groups=mesh['ctx'=8,'fsdp'=4] {'ctx','fsdp'}, use_global_device_ids=true, to_apply=%region_36.37.clone | all-reduce | flops 10752 | bytes 86016
  994.9 51.3 %reduce-scatter.18.cloned.1.call-done = f32[24,768]{1,0:T(8,128)} async-done(((f32[768,768]{1,0:T(8,128)}), f32[24,768]{1,0:T(8,128)}) %reduce-scatter.18.cloned.1.call-update) | async-done | bytes 73744 | tf_op jit(solution)/shard_map/reduce_scatter | solution.py:295
  1046.2 142.2 %reduce-scatter.20.cloned.1.call-done = f32[24,3072]{1,0:T(8,128)} async-done(((f32[768,3072]{1,0:T(8,128)}), f32[24,3072]{1,0:T(8,128)}) %reduce-scatter.20.cloned.1.call-update) | async-done | bytes 294928 | tf_op jit(solution)/shard_map/reduce_scatter | solution.py:296
  1188.4 140.8 %reduce-scatter.22.cloned.1.call-done = f32[96,768]{1,0:T(8,128)} async-done(((f32[3072,768]{1,0:T(8,128)}), f32[96,768]{1,0:T(8,128)}) %reduce-scatter.22.cloned.1.call-update) | async-done | bytes 294928 | tf_op jit(solution)/shard_map/reduce_scatter | solution.py:297
  1329.2 125.6 %reduce-scatter.16.cloned.1.call-done = f32[24,2304]{1,0:T(8,128)} async-done(((f32[768,2304]{1,0:T(8,128)}), f32[24,2304]{1,0:T(8,128)}) %reduce-scatter.16.cloned.1.call-update) | async-done | bytes 221200 | tf_op jit(solution)/shard_map/reduce_scatter | solution.py:294
  (371 shorter events, 267.5 us)
Async XLA Ops:
  7.2 75.3 %all-gather.10.cloned.1.call-start = ((), (), s32[]{:S(2)}) async-start(), calls=%async_computation.7 | async-start | bytes 4423680 | tf_op jit(solution)/shard_map/all_gather | solution.py:82
  7.9 126.4 %all-gather.12.cloned.1.call-start = ((), (), s32[]{:S(2)}) async-start(), calls=%async_computation.8 | async-start | bytes 7077888 | tf_op jit(solution)/shard_map/all_gather | solution.py:110
  35.4 51.5 %copy-start.26 = (f32[768]{0:T(1024)}, f32[768]{0:T(1024)S(1)}, u32[]{:S(2)}) copy-start(f32[768]{0:T(1024)S(1)} %get-tuple-element.379) | copy-start | bytes 9220
  36.0 50.9 %copy-start.39 = (f32[768]{0:T(1024)}, f32[768]{0:T(1024)S(1)}, u32[]{:S(2)}) copy-start(f32[768]{0:T(1024)S(1)} %get-tuple-element.376) | copy-start | bytes 9220
  36.0 349.6 %copy-start.43 = (f32[768]{0:T(1024)}, f32[768]{0:T(1024)S(1)}, u32[]{:S(2)}) copy-start(f32[768]{0:T(1024)S(1)} %get-tuple-element.373) | copy-start | bytes 9220
  36.0 353.9 %copy-start.41 = (f32[768]{0:T(1024)}, f32[768]{0:T(1024)S(1)}, u32[]{:S(2)}) copy-start(f32[768]{0:T(1024)S(1)} %get-tuple-element.371) | copy-start | bytes 9220
  37.3 49.5 %copy-start.28 = (f32[512]{0:T(512)}, f32[512]{0:T(512)S(1)}, u32[]{:S(2)}) copy-start(f32[512]{0:T(512)S(1)} %broadcast_multiply_fusion.4) | copy-start | bytes 6148
  38.8 48.0 %copy-start.32 = (f32[512]{0:T(512)}, f32[512]{0:T(512)S(1)}, u32[]{:S(2)}) copy-start(f32[512]{0:T(512)S(1)} %fusion.57) | copy-start | bytes 6148
  38.8 48.0 %copy-start.30 = (f32[512]{0:T(512)}, f32[512]{0:T(512)S(1)}, u32[]{:S(2)}) copy-start(f32[512]{0:T(512)S(1)} %fusion.83) | copy-start | bytes 6148
  90.1 5.0 copy-start.50
  90.1 5.2 copy-start.53
  90.1 5.7 copy-start.49
  90.1 19.4 %copy-start.51 = (bf16[768]{0:T(1024)(128)(2,1)S(1)}, bf16[768]{0:T(1024)(128)(2,1)}, u32[]{:S(2)}) copy-start(bf16[768]{0:T(1024)(128)(2,1)} %param.26) | copy-start | bytes 4612
  90.1 91.7 %all-gather.14.cloned.1.call-start = ((), (), s32[]{:S(2)}) async-start(), calls=%async_computation.9 | async-start | bytes 7077888 | tf_op jit(solution)/shard_map/all_gather | solution.py:111
  93.2 292.3 %all-gather.16.cloned.1.call-start = ((), (), s32[]{:S(2)}) async-start(), calls=%async_computation.10 | async-start | bytes 1474560 | tf_op jit(solution)/shard_map/all_gather | solution.py:83
  93.8 296.1 %all-gather.18.cloned.1.call-start = ((), (), s32[]{:S(2)}) async-start(), calls=%async_computation.11 | async-start | bytes 5898240 | tf_op jit(solution)/shard_map/all_gather | solution.py:84
  94.4 317.0 %all-gather.20.cloned.1.call-start = ((), (), s32[]{:S(2)}) async-start(), calls=%async_computation.12 | async-start | bytes 5898240 | tf_op jit(solution)/shard_map/all_gather | solution.py:85
  94.9 679.7 %reduce-scatter.14.cloned.1.call-start = ((), (), s32[]{:S(2)}) async-start(), calls=%async_computation.14 | async-start | bytes 7077888 | tf_op jit(solution)/shard_map/reduce_scatter | solution.py:265
  210.9 8.3 copy-start
  233.0 8.4 copy-start
  255.5 8.4 copy-start
  277.9 8.3 copy-start
  300.3 8.3 copy-start
  322.7 8.4 copy-start
  345.1 8.4 copy-start
  367.6 8.3 copy-start
  389.9 21.5 %copy-start.19 = (bf16[1,512,768]{2,1,0:T(8,128)(2,1)S(1)}, bf16[1,512,768]{2,1,0:T(8,128)(2,1)}, u32[]{:S(2)}) copy-start(bf16[1,512,768]{2,1,0:T(8,128)(2,1)} %param.17) | copy-start | bytes 2359300
  411.4 7.4 copy-start.5
  422.2 12.4 copy-start.11
  451.1 4.6 copy-start.2
  464.1 5.4 copy-start.1
  464.1 10.3 copy-start.3
  482.1 4.6 copy-start.2
  495.1 5.9 copy-start.1
  495.1 10.6 copy-start.3
  513.5 4.6 copy-start.2
  526.5 5.9 copy-start.1
  526.5 10.6 copy-start.3
  544.8 4.6 copy-start.2
  557.9 5.9 copy-start.1
  557.9 10.6 copy-start.3
  576.2 4.6 copy-start.2
  589.3 5.9 copy-start.1
  589.3 10.6 copy-start.3
  620.6 5.9 copy-start.1
  620.6 10.7 copy-start.3
  652.0 5.9 copy-start.1
  652.0 10.7 copy-start.3
  683.4 5.9 copy-start.1
  683.4 10.6 copy-start.3
  712.4 127.7 %reduce-scatter.12.cloned.1.call-start = ((), (), s32[]{:S(2)}) async-start(), calls=%async_computation.13 | async-start | bytes 7077888 | tf_op jit(solution)/shard_map/reduce_scatter | solution.py:262
  727.0 215.4 %reduce-scatter.24.cloned.1.call-start = ((), (), s32[]{:S(2)}) async-start(), calls=%async_computation.19 | async-start | bytes 1622016
  729.4 316.8 %reduce-scatter.18.cloned.1.call-start = ((), (), s32[]{:S(2)}) async-start(), calls=%async_computation.16 | async-start | bytes 2433024 | tf_op jit(solution)/shard_map/reduce_scatter | solution.py:295
  733.2 455.3 %reduce-scatter.20.cloned.1.call-start = ((), (), s32[]{:S(2)}) async-start(), calls=%async_computation.17 | async-start | bytes 9732096 | tf_op jit(solution)/shard_map/reduce_scatter | solution.py:296
  740.5 588.7 %reduce-scatter.22.cloned.1.call-start = ((), (), s32[]{:S(2)}) async-start(), calls=%async_computation.18 | async-start | bytes 9732096 | tf_op jit(solution)/shard_map/reduce_scatter | solution.py:297
  748.6 91.6 %copy-start.9 = (bf16[1,512,768]{2,1,0:T(8,128)(2,1)S(1)}, bf16[1,512,768]{2,1,0:T(8,128)(2,1)}, u32[]{:S(2)}) copy-start(bf16[1,512,768]{2,1,0:T(8,128)(2,1)} %param.16) | copy-start | bytes 2359300
  748.6 91.6 %copy-start.27 = (f32[768]{0:T(1024)S(1)}, f32[768]{0:T(1024)}, u32[]{:S(2)}) copy-start(f32[768]{0:T(1024)} %copy-done.26) | copy-start | bytes 9220
  748.6 91.6 %copy-start.29 = (f32[512]{0:T(512)S(1)}, f32[512]{0:T(512)}, u32[]{:S(2)}) copy-start(f32[512]{0:T(512)} %copy-done.28) | copy-start | bytes 6148
  748.6 91.6 %copy-start.31 = (f32[512]{0:T(512)S(1)}, f32[512]{0:T(512)}, u32[]{:S(2)}) copy-start(f32[512]{0:T(512)} %copy-done.30) | copy-start | bytes 6148
  748.6 91.6 %copy-start.40 = (f32[768]{0:T(1024)S(1)}, f32[768]{0:T(1024)}, u32[]{:S(2)}) copy-start(f32[768]{0:T(1024)} %copy-done.39) | copy-start | bytes 9220
  748.6 706.2 %reduce-scatter.16.cloned.1.call-start = ((), (), s32[]{:S(2)}) async-start(), calls=%async_computation.15 | async-start | bytes 7299072 | tf_op jit(solution)/shard_map/reduce_scatter | solution.py:294
  943.8 4.9 copy-start.33
  943.8 5.8 copy-start.21
  943.8 5.8 copy-start.23
  (31 other events, 69.5 us)
Sparse Core Ops, SparseCore 0:
  9.6 72.8 all-gather.9
  90.2 44.0 all-gather.11
  136.2 45.5 all-gather.13
  183.2 30.4 all-gather.15
  215.1 88.5 all-gather.17
  305.1 87.8 all-gather.19
  712.5 62.0 reduce-scatter.13
  778.4 61.7 reduce-scatter.11
  845.4 96.9 reduce-scatter.23
  948.1 98.0 reduce-scatter.17
  1053.7 134.6 reduce-scatter.19
  1194.8 134.4 reduce-scatter.21
  1336.4 118.3 reduce-scatter.15
where the time goes:
time: 1470 us; the launch traced here: 1460 us
  waiting for transfers between devices  720 us (49%)
  matrix products  403 us (27%)
  local copies, waits for them, and re-layouts  131 us (9%)
  other arithmetic  96.1 us (7%)
  blocking collectives  94.5 us (6%)
  between operations  14.9 us (1%)
    reduce_scatter x1, waiting for transfers between devices, local(): lax.psum_scatter(grad_in_w, ('ctx', 'fsdp'), scatter_dimension=0, tiled=T...  142 us
    reduce_scatter x1, waiting for transfers between devices, local(): lax.psum_scatter(grad_back_w, ('ctx', 'fsdp'), scatter_dimension=0, tiled...  141 us
    reduce_scatter x1, waiting for transfers between devices, local(): lax.psum_scatter(grad_qkv_w, ('ctx', 'fsdp'), scatter_dimension=0, tiled=...  126 us
    unnamed x14, waiting for transfers between devices  89.8 us
    dot_general x8, matrix products, grad_pair(): jnp.einsum('qhd,khd->hqk', grad_rows, value3, preferred_element_type=jnp....  67.5 us
    reduce_scatter x1, waiting for transfers between devices, local(): lax.psum_scatter(key_terms.astype(jnp.bfloat16), 'ctx', scatter_dimension...  65.5 us
    dot_general x8, matrix products, visit_block(): jnp.einsum('qhd,khd->hqk', query3, key3, preferred_element_type=jnp.float32)  64 us
    reduce_sum x8, other arithmetic, visit_block(): totals = totals * rescale + jnp.sum(expo, axis=-1)  61.3 us
  transfers between devices with their start and end apart: 13, of which 10 were waited for; matrix products, arithmetic and copies ran while one was open for 21% of the time, Pallas kernels for 0%

commit v1 on v0

--- a/solution.py
+++ b/solution.py
@@ -7,6 +7,11 @@
 D = 768
 H = 12
 DH = 64
+link_cubes = lambda chunk, z: jnp.split(
+    lax.all_gather(jnp.concatenate([chunk, z], 1), "ctx", axis=0, tiled=True),
+    [chunk.shape[1]],
+    axis=1,
+)
 
 
 def layer_norm(values, gain, shift):
@@ -107,8 +112,7 @@
         jnp.zeros((H, tok_rows), jnp.float32),
         jnp.zeros((H, tok_rows, DH), jnp.float32),
     )
-    key_rows = lax.all_gather(keyed, "ctx", axis=0, tiled=True)
-    value_rows = lax.all_gather(valued, "ctx", axis=0, tiled=True)
+    key_rows, value_rows = link_cubes(keyed, valued)
     key_count = key_rows.shape[0]
     block_rows = 512
     block_count = key_count // block_rows

time: 1470 us -> 1570 us (1.068)
  local copies, waits for them, and re-layouts: 131 us -> 185 us
  waiting for transfers between devices: 720 us -> 770 us
    all_gather x2 -> x3, waiting for transfers between devices: 36.6 us -> 86.3 us  [the longest x1 52.2 us: lax.all_gather(jnp.concatenate([chunk, z], 1), 'ctx', axis=0, tiled=True)]
    split x0 -> x3, local copies, waits for them, and re-layouts: none -> 28.2 us  [jnp.split(lax.all_gather(jnp.concatenate([chunk, z], 1), 'ctx', axis=0, t...]
    unnamed x112 -> x120, local copies, waits for them, and re-layouts: 54 us -> 78.9 us
    unnamed x14 -> x15, waiting for transfers between devices: 89.8 us -> 89.9 us
  transfers between devices with their start and end apart: 13 -> 14, of which waited for: 10 -> 11; matrix products, arithmetic and copies ran while one was open for 21% -> 23% of each run, Pallas kernels for 0% -> 0%
where the time goes in v1:
time: 1570 us
  waiting for transfers between devices  770 us (49%)
  matrix products  403 us (26%)
  local copies, waits for them, and re-layouts  185 us (12%)
  other arithmetic  99.1 us (6%)
  blocking collectives  94.2 us (6%)
    reduce_scatter x1, waiting for transfers between devices, local(): lax.psum_scatter(grad_in_w, ('ctx', 'fsdp'), scatter_dimension=0, tiled=T...  142 us
    reduce_scatter x1, waiting for transfers between devices, local(): lax.psum_scatter(grad_back_w, ('ctx', 'fsdp'), scatter_dimension=0, tiled...  141 us
    reduce_scatter x1, waiting for transfers between devices, local(): lax.psum_scatter(grad_qkv_w, ('ctx', 'fsdp'), scatter_dimension=0, tiled=...  125 us
    unnamed x15, waiting for transfers between devices  89.9 us
    unnamed x120, local copies, waits for them, and re-layouts  78.9 us
    dot_general x8, matrix products, grad_pair(): jnp.einsum('qhd,khd->hqk', grad_rows, value3, preferred_element_type=jnp....  67.5 us
    reduce_scatter x1, waiting for transfers between devices, local(): lax.psum_scatter(key_terms.astype(jnp.bfloat16), 'ctx', scatter_dimension...  65.6 us
    dot_general x8, matrix products, visit_block(): jnp.einsum('qhd,khd->hqk', query3, key3, preferred_element_type=jnp.float32)  64 us
  transfers between devices with their start and end apart: 14, of which 11 were waited for; matrix products, arithmetic and copies ran while one was open for 23% of the time, Pallas kernels for 0%

profile of v1, /device:TPU:0, one launch (start us, length us, event | category | flops | bytes accessed | tf_op | source)
XLA Modules:
  0.0 1568.3 jit_solution(6162188369739779520)
XLA Ops:
  8.0 14.9 all-gather.1
  23.0 12.2 all-gather
  38.9 43.6 %all-gather.11.cloned.1.call-done = bf16[768,2304]{1,0:T(8,128)(2,1)} async-done(((bf16[192,2304]{1,0:T(8,128)(2,1)}), bf16[768,2304]{1,0:T(8,128)(2,1)}) %all-gather.11.cloned.1.call-update) | async-done | bytes 3538960 | tf_op jit(solution)/shard_map/all_gather | solution.py:87
  98.4 13.0 all_gather.45
  112.1 13.3 all-gather.2
  127.2 7.0 all-gather.21.cloned.1.call-done
  134.2 8.6 copy.103
  142.8 7.5 copy.130
  155.2 27.0 %all-gather.23.cloned.1.call-done = bf16[4096,768]{1,0:T(8,128)(2,1)} async-done(((bf16[512,768]{1,0:T(8,128)(2,1)}), bf16[4096,768]{1,0:T(8,128)(2,1)}) %all-gather.23.cloned.1.call-update) | async-done | bytes 6291472 | tf_op jit(solution)/shard_map/all_gather | solution.py:241
  182.3 9.1 copy.104
  191.4 7.7 copy.131
  204.0 52.2 %all-gather.13.cloned.1.call-done = bf16[4096,1536]{1,0:T(8,128)(2,1)} async-done(((bf16[512,1536]{1,0:T(8,128)(2,1)}), bf16[4096,1536]{1,0:T(8,128)(2,1)}) %all-gather.13.cloned.1.call-update) | async-done | bytes 12582928 | tf_op jit(solution)/shard_map/all_gather | solution.py:11
  256.2 10.4 fusion.104
  266.5 8.9 copy.97
  275.5 7.0 copy.128
  287.3 8.9 copy.99
  296.2 7.4 copy.129
  308.6 180.4 %while.30 = (s32[]{:T(128)}, f32[12,512]{1,0:T(8,128)S(1)}, f32[12,512]{1,0:T(8,128)S(1)}, f32[12,512,64]{1,2,0:T(8,128)}, s32[8,512]{1,0:T(8,128)S(1)}, /*index...) while((s32[]{:T(128)}, f32[12,512]{1,0:T(8,128)S(1)}, ...), condition=%wide.region_10.11_spmd.clone, body=%wide.region_7.10_spmd.clone.sunk | while | flops 848197632 | bytes 95043760 | solution.py:144
  308.9 8.0 fusion.151
  316.9 7.7 fusion.152
  331.1 8.0 fusion.151
  339.1 7.7 fusion.152
  353.6 8.0 fusion.151
  361.6 7.7 fusion.152
  375.9 8.0 fusion.151
  383.9 7.8 fusion.152
  399.3 8.0 fusion.151
  407.3 7.7 fusion.152
  421.7 8.0 fusion.151
  429.8 7.6 fusion.152
  444.2 8.0 fusion.151
  452.2 7.7 fusion.152
  466.5 8.0 fusion.151
  474.6 7.7 fusion.152
  497.0 21.5 %fusion.101 = (f32[512]{0:T(512)S(1)}, f32[512,3072]{1,0:T(8,128)}, f32[512,3072]{1,0:T(8,128)}, f32[512,3072]{1,0:T(8,128)}) fusion(f32[3072]{0:T(1024)S(1)} %bitcast.275, bf16[768,3072]{1,0:T(8,128)(2,1)} %all-gather.17.cloned.1.call-done, f32[512,768]{1,0:T(8,128)} %copy-done.11, f32[768]{0:T(1024)S(1)} %get-tuple-element.371, ...), kind=kOutput, calls=%fused_computation.206 | convolution fusion | flops 2521693696 | bytes 25190400 | tf_op jit(solution)/shard_map/dot_general | solution.py:154
  518.5 7.4 multiply_reduce_fusion.1
  529.3 10.6 convert_reduce_fusion
  541.5 6.0 multiply_reduce_fusion.3
  554.7 251.2 %while.31 = (s32[]{:T(128)}, f32[512,12,64]{0,2,1:T(8,128)}, bf16[8,512,12,64]{1,3,2,0:T(8,128)(2,1)}, bf16[8,512,12,64]{1,3,2,0:T(8,128)(2,1)}, bf16[8,512,12,6...) while((s32[]{:T(128)}, f32[512,12,64]{0,2,1:T(8,128)}, ...), condition=%wide.region_24.25_spmd.clone, body=%wide.region_23.24_spmd.clone.sunk | while | flops 2047082496 | bytes 195125520 | solution.py:253
  562.7 8.4 fusion.166
  593.7 8.4 fusion.166
  625.1 8.4 fusion.166
  656.4 8.4 fusion.166
  664.9 5.9 bitcast_add_fusion.2
  687.8 8.4 fusion.166
  719.1 8.4 fusion.166
  750.5 8.4 fusion.166
  781.9 8.4 fusion.166
  805.9 6.9 copy.109
  812.8 6.8 copy.133
  819.8 6.9 copy.108
  826.8 7.2 copy.132
  840.2 7.2 fusion.95
  849.3 6.2 fusion.66
  857.2 24.6 %reduce-scatter.14.cloned.1.call-done = bf16[512,768]{0,1:T(8,128)(2,1)} async-done(((bf16[4096,768]{0,1:T(8,128)(2,1)}), bf16[512,768]{0,1:T(8,128)(2,1)}) %reduce-scatter.14.cloned.1.call-update) | async-done | bytes 786448 | tf_op jit(solution)/shard_map/reduce_scatter | solution.py:269
  881.7 65.6 %reduce-scatter.12.cloned.1.call-done = bf16[512,768]{0,1:T(8,128)(2,1)} async-done(((bf16[4096,768]{0,1:T(8,128)(2,1)}), bf16[512,768]{0,1:T(8,128)(2,1)}) %reduce-scatter.12.cloned.1.call-update) | async-done | bytes 786448 | tf_op jit(solution)/shard_map/reduce_scatter | solution.py:266
  947.3 6.6 fusion.88
  955.3 6.8 fusion.64
  962.1 87.3 %reduce-scatter.24.cloned.1.call-done = f32[96,2]{1,0:T(8,128)} async-done(((f32[3072,2]{1,0:T(8,128)}), f32[96,2]{1,0:T(8,128)}) %reduce-scatter.24.cloned.1.call-update) | async-done | bytes 784
  1059.3 40.7 %all-reduce.3 = (f32[3,768]{1,0:T(4,128)S(1)}, f32[7,768]{1,0:T(8,128)S(1)}, f32[3072]{0:T(1024)S(1)}) all-reduce(f32[3,768]{1,0:T(4,128)S(1)} %pad_maximum_fusion.3, f32[7,768]{1,0:T(8,128)S(1)} %stack.36, f32[3072]{0:T(1024)S(1)} %copy-done.27), channel_id=8, replica_groups=mesh['ctx'=8,'fsdp'=4] {'ctx','fsdp'}, use_global_device_ids=true, to_apply=%region_36.37.clone | all-reduce | flops 10752 | bytes 86016
  1101.9 51.4 %reduce-scatter.18.cloned.1.call-done = f32[24,768]{1,0:T(8,128)} async-done(((f32[768,768]{1,0:T(8,128)}), f32[24,768]{1,0:T(8,128)}) %reduce-scatter.18.cloned.1.call-update) | async-done | bytes 73744 | tf_op jit(solution)/shard_map/reduce_scatter | solution.py:299
  1153.3 141.9 %reduce-scatter.20.cloned.1.call-done = f32[24,3072]{1,0:T(8,128)} async-done(((f32[768,3072]{1,0:T(8,128)}), f32[24,3072]{1,0:T(8,128)}) %reduce-scatter.20.cloned.1.call-update) | async-done | bytes 294928 | tf_op jit(solution)/shard_map/reduce_scatter | solution.py:300
  1295.2 141.1 %reduce-scatter.22.cloned.1.call-done = f32[96,768]{1,0:T(8,128)} async-done(((f32[3072,768]{1,0:T(8,128)}), f32[96,768]{1,0:T(8,128)}) %reduce-scatter.22.cloned.1.call-update) | async-done | bytes 294928 | tf_op jit(solution)/shard_map/reduce_scatter | solution.py:301
  1436.3 125.3 %reduce-scatter.16.cloned.1.call-done = f32[24,2304]{1,0:T(8,128)} async-done(((f32[768,2304]{1,0:T(8,128)}), f32[24,2304]{1,0:T(8,128)}) %reduce-scatter.16.cloned.1.call-update) | async-done | bytes 221200 | tf_op jit(solution)/shard_map/reduce_scatter | solution.py:298
  (386 shorter events, 316.1 us)
Async XLA Ops:
  7.2 75.3 %all-gather.11.cloned.1.call-start = ((), (), s32[]{:S(2)}) async-start(), calls=%async_computation.7 | async-start | bytes 4423680 | tf_op jit(solution)/shard_map/all_gather | solution.py:87
  7.9 126.3 %all-gather.21.cloned.1.call-start = ((), (), s32[]{:S(2)}) async-start(), calls=%async_computation.12 | async-start | bytes 7077888 | tf_op jit(solution)/shard_map/all_gather | solution.py:240
  35.4 51.5 %copy-start.28 = (f32[768]{0:T(1024)}, f32[768]{0:T(1024)S(1)}, u32[]{:S(2)}) copy-start(f32[768]{0:T(1024)S(1)} %get-tuple-element.379) | copy-start | bytes 9220
  36.0 50.9 %copy-start.41 = (f32[768]{0:T(1024)}, f32[768]{0:T(1024)S(1)}, u32[]{:S(2)}) copy-start(f32[768]{0:T(1024)S(1)} %get-tuple-element.376) | copy-start | bytes 9220
  36.0 456.7 %copy-start.45 = (f32[768]{0:T(1024)}, f32[768]{0:T(1024)S(1)}, u32[]{:S(2)}) copy-start(f32[768]{0:T(1024)S(1)} %get-tuple-element.373) | copy-start | bytes 9220
  36.0 461.0 %copy-start.43 = (f32[768]{0:T(1024)}, f32[768]{0:T(1024)S(1)}, u32[]{:S(2)}) copy-start(f32[768]{0:T(1024)S(1)} %get-tuple-element.371) | copy-start | bytes 9220
  37.3 49.5 %copy-start.30 = (f32[512]{0:T(512)}, f32[512]{0:T(512)S(1)}, u32[]{:S(2)}) copy-start(f32[512]{0:T(512)S(1)} %broadcast_multiply_fusion.4) | copy-start | bytes 6148
  38.8 48.0 %copy-start.34 = (f32[512]{0:T(512)}, f32[512]{0:T(512)S(1)}, u32[]{:S(2)}) copy-start(f32[512]{0:T(512)S(1)} %fusion.57) | copy-start | bytes 6148
  38.8 48.0 %copy-start.32 = (f32[512]{0:T(512)}, f32[512]{0:T(512)S(1)}, u32[]{:S(2)}) copy-start(f32[512]{0:T(512)S(1)} %fusion.83) | copy-start | bytes 6148
  90.0 92.2 %all-gather.23.cloned.1.call-start = ((), (), s32[]{:S(2)}) async-start(), calls=%async_computation.13 | async-start | bytes 7077888 | tf_op jit(solution)/shard_map/all_gather | solution.py:241
  93.1 4.6 copy-start.52
  93.1 4.7 copy-start.55
  93.1 5.3 copy-start.51
  93.1 19.0 %copy-start.53 = (bf16[768]{0:T(1024)(128)(2,1)S(1)}, bf16[768]{0:T(1024)(128)(2,1)}, u32[]{:S(2)}) copy-start(bf16[768]{0:T(1024)(128)(2,1)} %param.26) | copy-start | bytes 4612
  93.2 163.0 %all-gather.13.cloned.1.call-start = ((), (), s32[]{:S(2)}) async-start(), calls=%async_computation.8 | async-start | bytes 14155776 | tf_op jit(solution)/shard_map/all_gather | solution.py:11
  95.7 397.0 %all-gather.15.cloned.1.call-start = ((), (), s32[]{:S(2)}) async-start(), calls=%async_computation.9 | async-start | bytes 1474560 | tf_op jit(solution)/shard_map/all_gather | solution.py:88
  96.3 400.7 %all-gather.17.cloned.1.call-start = ((), (), s32[]{:S(2)}) async-start(), calls=%async_computation.10 | async-start | bytes 5898240 | tf_op jit(solution)/shard_map/all_gather | solution.py:89
  96.8 421.7 %all-gather.19.cloned.1.call-start = ((), (), s32[]{:S(2)}) async-start(), calls=%async_computation.11 | async-start | bytes 5898240 | tf_op jit(solution)/shard_map/all_gather | solution.py:90
  97.6 784.1 %reduce-scatter.14.cloned.1.call-start = ((), (), s32[]{:S(2)}) async-start(), calls=%async_computation.15 | async-start | bytes 7077888 | tf_op jit(solution)/shard_map/reduce_scatter | solution.py:269
  316.9 8.4 copy-start
  339.1 8.4 copy-start
  361.6 8.3 copy-start
  383.9 9.3 copy-start
  407.3 8.4 copy-start
  429.7 8.4 copy-start
  452.2 8.3 copy-start
  474.6 8.3 copy-start
  497.0 21.5 %copy-start.20 = (bf16[1,512,768]{2,1,0:T(8,128)(2,1)S(1)}, bf16[1,512,768]{2,1,0:T(8,128)(2,1)}, u32[]{:S(2)}) copy-start(bf16[1,512,768]{2,1,0:T(8,128)(2,1)} %param.17) | copy-start | bytes 2359300
  497.0 21.5 %copy-start.25 = (f32[4,1,768]{2,1,0:T(1,128)S(1)}, f32[4,1,768]{2,1,0:T(1,128)}, u32[]{:S(2)}) copy-start(f32[4,1,768]{2,1,0:T(1,128)} %convert_element_type.127) | copy-start | bytes 36868
  518.5 7.4 copy-start.5
  529.3 12.2 copy-start.12
  558.1 4.6 copy-start.2
  571.1 5.4 copy-start.1
  571.1 10.3 copy-start.3
  589.1 4.6 copy-start.2
  602.1 5.9 copy-start.1
  602.1 10.6 copy-start.3
  620.5 4.6 copy-start.2
  633.5 5.9 copy-start.1
  633.5 10.6 copy-start.3
  664.9 5.9 copy-start.1
  664.9 10.6 copy-start.3
  696.2 5.9 copy-start.1
  696.2 10.6 copy-start.3
  727.6 5.9 copy-start.1
  727.6 10.7 copy-start.3
  759.0 5.9 copy-start.1
  759.0 10.7 copy-start.3
  790.4 5.9 copy-start.1
  790.4 10.6 copy-start.3
  819.6 127.6 %reduce-scatter.12.cloned.1.call-start = ((), (), s32[]{:S(2)}) async-start(), calls=%async_computation.14 | async-start | bytes 7077888 | tf_op jit(solution)/shard_map/reduce_scatter | solution.py:266
  834.0 215.4 %reduce-scatter.24.cloned.1.call-start = ((), (), s32[]{:S(2)}) async-start(), calls=%async_computation.20 | async-start | bytes 1622016
  836.4 316.8 %reduce-scatter.18.cloned.1.call-start = ((), (), s32[]{:S(2)}) async-start(), calls=%async_computation.17 | async-start | bytes 2433024 | tf_op jit(solution)/shard_map/reduce_scatter | solution.py:299
  840.2 455.0 %reduce-scatter.20.cloned.1.call-start = ((), (), s32[]{:S(2)}) async-start(), calls=%async_computation.18 | async-start | bytes 9732096 | tf_op jit(solution)/shard_map/reduce_scatter | solution.py:300
  847.5 588.8 %reduce-scatter.22.cloned.1.call-start = ((), (), s32[]{:S(2)}) async-start(), calls=%async_computation.19 | async-start | bytes 9732096 | tf_op jit(solution)/shard_map/reduce_scatter | solution.py:301
  855.6 91.7 %copy-start.9 = (bf16[1,512,768]{2,1,0:T(8,128)(2,1)S(1)}, bf16[1,512,768]{2,1,0:T(8,128)(2,1)}, u32[]{:S(2)}) copy-start(bf16[1,512,768]{2,1,0:T(8,128)(2,1)} %param.16) | copy-start | bytes 2359300
  855.6 91.7 %copy-start.29 = (f32[768]{0:T(1024)S(1)}, f32[768]{0:T(1024)}, u32[]{:S(2)}) copy-start(f32[768]{0:T(1024)} %copy-done.28) | copy-start | bytes 9220
  855.6 91.7 %copy-start.31 = (f32[512]{0:T(512)S(1)}, f32[512]{0:T(512)}, u32[]{:S(2)}) copy-start(f32[512]{0:T(512)} %copy-done.30) | copy-start | bytes 6148
  855.6 91.7 %copy-start.33 = (f32[512]{0:T(512)S(1)}, f32[512]{0:T(512)}, u32[]{:S(2)}) copy-start(f32[512]{0:T(512)} %copy-done.32) | copy-start | bytes 6148
  855.6 91.7 %copy-start.42 = (f32[768]{0:T(1024)S(1)}, f32[768]{0:T(1024)}, u32[]{:S(2)}) copy-start(f32[768]{0:T(1024)} %copy-done.41) | copy-start | bytes 9220
  855.6 706.0 %reduce-scatter.16.cloned.1.call-start = ((), (), s32[]{:S(2)}) async-start(), calls=%async_computation.16 | async-start | bytes 7299072 | tf_op jit(solution)/shard_map/reduce_scatter | solution.py:298
  1050.8 4.9 copy-start.35
  1050.8 5.8 copy-start.22
  1050.8 5.8 copy-start.24
  (34 other events, 81.7 us)
Sparse Core Ops, SparseCore 0:
  9.6 72.8 all-gather.10
  90.1 44.0 all-gather.20
  136.7 45.5 all-gather.22
  184.0 72.1 all-gather.12
  257.6 30.4 all-gather.14
  289.5 88.5 all-gather.16
  379.6 87.8 all-gather.18
  819.7 61.9 reduce-scatter.13
  885.5 61.7 reduce-scatter.11
  952.4 96.9 reduce-scatter.23
  1055.3 97.9 reduce-scatter.17
  1160.6 134.5 reduce-scatter.19
  1301.6 134.6 reduce-scatter.21
  1443.3 118.1 reduce-scatter.15
